TPU v7x, 32 devices: a whole 2x2x4 slice. The times are simulated.
32 devices in a mesh: dir: 8 (over z, y), near: 4 (over x, core).
Axes of the slice: x: 2, y: 2, z: 4, core: 2. Of those that a mesh axis runs over, the one named last changes fastest.
Arguments:
- currents: bfloat16 [1024, 128, 128], P(('dir', 'near')), may hold values from -6 to 6
- counts: int32 [32], replicated, may hold values from 0 to 4, as said below
- near_source: int32 [1024, 6], P(('dir', 'near')), may hold values from 0 to 1023, as said below
- near_blocks: bfloat16 [1024, 6, 128, 256], P(('dir', 'near')), may hold values from -0.15625 to 0.15625
- aggregate: bfloat16 [8, 1152, 256], replicated, may hold values from -0.125 to 0.125
- receive: bfloat16 [8, 128, 2304], replicated, may hold values from -0.125 to 0.125
- translations: bfloat16 [1, 1, 1152, 64, 128], P(None, None, ('dir', 'near')), may hold values from -0.5 to 0.5
- source_blocks: int32 [1, 1], replicated, may hold values from 0 to 0, as said below
Outputs:
- fields: bfloat16 [1024, 128, 128], P(('dir', 'near'))
Inputs may be any that keep to these rules, and one draw needn't show every extreme that they name: `counts`: devices 2 m and 2 m + 1 of dir and near together (neighbours along near) own exactly 4 parents between them; some device owns 4 and its neighbour none. `near_source`: every entry names a live leaf slot on the device of its row or on a device next to it along near with the same dir index. `source_blocks`: each row names 1 different blocks.
All inputs are finite; a program needn't handle non-finite values.
Results may differ from a plain program's by a relative error of at most 0.005.
Values may be sent and summed in bfloat16 or wider, within the bound.
A program may use at most 128 MiB of HBM per device.

v0:
```python
import jax
import jax.numpy as jnp
from jax import lax
from jax.sharding import PartitionSpec as P


def partner(value, axis, stride):
    mask = 2**stride
    pairs = [(source, source ^ mask) for source in range(lax.axis_size(axis))]
    return lax.ppermute(value, axis, pairs)


def padded(cells, sides, width):
    for axis, dim in sides:
        count = lax.axis_size(axis)
        ends = count - 1
        head = lax.slice_in_dim(cells, 0, width, axis=dim)
        tail = lax.slice_in_dim(cells, cells.shape[dim] - width, cells.shape[dim], axis=dim)
        cells = jnp.concatenate(
            [
                lax.ppermute(tail, axis, [(i, (i + 1) % count) for i in range(ends)]),
                cells,
                lax.ppermute(head, axis, [((i + 1) % count, i) for i in range(ends)]),
            ],
            axis=dim,
        )
    return cells


def turned(values):
    middle = values.shape[-1] // 2
    return jnp.concatenate([-values[..., middle:], values[..., :middle]], axis=-1)


def regroup(patterns, slot_count):
    groups = lax.axis_size(("dir", "near"))
    channels = patterns.shape[-1]
    per_group = patterns.shape[1] // groups
    shaped = patterns.reshape(1, slot_count, groups, per_group, channels)
    exchanged = lax.all_to_all(shaped, ("dir", "near"), split_axis=2, concat_axis=0, tiled=True)
    return exchanged.reshape(groups * slot_count, per_group, channels)


def collect(fields, slot_count):
    groups = lax.axis_size(("dir", "near"))
    channels = fields.shape[-1]
    per_group = fields.shape[1]
    shaped = fields.reshape(groups, slot_count, 1, per_group, channels)
    exchanged = lax.all_to_all(shaped, ("dir", "near"), split_axis=0, concat_axis=2, tiled=True)
    return exchanged.reshape(slot_count, groups * per_group, channels)


def translate(ordered, translations, source_blocks):
    block_count, list_length, per_group, block_size, doubled_size = translations.shape
    channels = ordered.shape[-1]
    blocks = ordered.reshape(block_count, block_size, per_group, channels)
    with_turned = jnp.concatenate([blocks, turned(blocks)], axis=1)
    sources = with_turned[source_blocks]
    summed = jnp.einsum(
        "tlkij,tljkr->tikr", translations, sources, preferred_element_type=jnp.float32
    )
    return summed.astype(jnp.bfloat16).reshape(block_count * block_size, per_group, channels)


def body(
    currents, counts, near_source, near_blocks, aggregate, receive, translations, source_blocks
):
    groups = lax.axis_size(("dir", "near"))
    device_index = lax.axis_index(("dir", "near"))
    leaf_slots, unknowns, channels = currents.shape
    parent_slots = leaf_slots // 8
    half_slots = parent_slots // 2
    parents = translations.shape[0] * translations.shape[3]
    starts = jnp.cumsum(counts) - counts
    own_count = counts[device_index]
    children = currents.reshape(parent_slots, 8, unknowns, channels)
    spare_rows = partner(children[half_slots:], "near", 0)
    chosen_rows = []
    for slot_index in range(half_slots):
        offset_index = jnp.clip(slot_index - own_count, 0, half_slots - 1)
        borrowed = lax.dynamic_index_in_dim(spare_rows, offset_index, 0, keepdims=False)
        chosen_rows.append(jnp.where(slot_index < own_count, children[slot_index], borrowed))
    worked = jnp.stack(chosen_rows)
    work_slots = worked.shape[0]
    stacked = jnp.concatenate([worked, turned(worked)], axis=2)
    patterns = jnp.einsum(
        "ckq,scqr->skr", aggregate, stacked, preferred_element_type=jnp.float32
    ).astype(jnp.bfloat16)
    gathered = regroup(patterns, work_slots)
    parent_ids = jnp.arange(parents, dtype=jnp.int32)
    range_ends = jnp.cumsum(counts)
    before = (range_ends[None, :] <= parent_ids[:, None]).astype(jnp.int32)
    owners = jnp.sum(before, axis=1)
    local_slot = parent_ids - jnp.sum(before * counts[None, :], axis=1)
    device_ids = jnp.arange(groups, dtype=jnp.int32)
    slot_ids = jnp.arange(work_slots, dtype=jnp.int32)[None, :]
    partners = jnp.bitwise_xor(owners, 1)
    partner_count = jnp.sum(
        jnp.where(device_ids[None, :] == partners[:, None], counts[None, :], 0), axis=1
    )
    position = jnp.where(
        local_slot < half_slots,
        owners * half_slots + local_slot,
        partners * half_slots + partner_count + local_slot - half_slots,
    )
    partner_starts = starts.reshape(-1, 2)[:, ::-1].reshape(-1)
    anchor = jnp.where(
        slot_ids < counts[:, None],
        starts[:, None] + slot_ids,
        partner_starts[:, None] + half_slots + slot_ids - counts[:, None],
    )
    incoming = translate(gathered[position], translations, source_blocks)
    anchor = jnp.clip(anchor, 0, parents - 1).reshape(-1)
    returned = collect(incoming[anchor], work_slots)
    doubled = jnp.concatenate([returned, turned(returned)], axis=1)
    far_field = jnp.einsum("cpk,skr->scpr", receive, doubled, preferred_element_type=jnp.float32)
    far_back = partner(far_field.astype(jnp.bfloat16), "near", 0).astype(far_field.dtype)
    partner_own = counts[jnp.bitwise_xor(device_index, 1)]
    far_rows = [far_field[slot_index] for slot_index in range(half_slots)]
    for slot_index in range(half_slots, parent_slots):
        offset_index = jnp.clip(partner_own + slot_index - half_slots, 0, half_slots - 1)
        far_rows.append(lax.dynamic_index_in_dim(far_back, offset_index, 0, keepdims=False))
    far_field = jnp.stack(far_rows)
    window = padded(currents, (("near", 0),), leaf_slots)
    window_start = (device_index - 1) * leaf_slots
    sources = window[near_source - window_start]
    with_turned = jnp.concatenate([sources, turned(sources)], axis=2)
    near_field = jnp.einsum(
        "ienq,ieqr->inr", near_blocks, with_turned, preferred_element_type=jnp.float32
    )
    summed = far_field.reshape(leaf_slots, unknowns, channels) + near_field
    is_live = jnp.arange(leaf_slots) // 8 < own_count
    return jnp.where(is_live[:, None, None], summed, 0.0).astype(jnp.bfloat16)


def solution(mesh):
    return jax.shard_map(
        body,
        mesh=mesh,
        in_specs=(
            P(("dir", "near"), None, None),
            P(),
            P(("dir", "near"), None),
            P(("dir", "near"), None, None, None),
            P(),
            P(),
            P(None, None, ("dir", "near"), None, None),
            P(),
        ),
        out_specs=P(("dir", "near"), None, None),
        check_vma=False,
    )
```

profile of v0, /device:TPU:0, one launch (start us, length us, event | category | flops | bytes accessed | tf_op | source)
XLA Modules:
  0.0 108.1 jit_solution(5757620618695763654)
XLA Ops:
  0.0 1.1 %slice.42 = bf16[16,128,128]{2,1,0:T(8,128)(2,1)S(1)} slice(bf16[32,128,128]{2,1,0:T(8,128)(2,1)} %param.8), slice={[16:32], [0:128], [0:128]} | slice | bytes 1048576 | tf_op jit(solution)/shard_map/slice | solution.py:77
  1.1 0.3 copy.50
  1.4 0.6 collective-permute-start
  2.0 1.4 %fusion.56 = (s32[1]{0:T(128)}, s32[1]{0:T(128)}) fusion(s32[32]{0:T(128)} %param.9, s32[]{:T(128)S(6)} %select_n.106, s32[]{:T(128)S(6)} %select_n.95), kind=kLoop, calls=%fused_computation.87 | loop fusion | bytes 24 | tf_op jit(solution)/shard_map/dynamic_slice | solution.py:118
  5.7 1.1 fusion.55
  6.7 0.2 copy.69
  6.9 0.2 copy.70
  7.3 3.9 %fusion.16 = bf16[2,1152,128]{1,2,0:T(8,128)(2,1)S(1)} fusion(bf16[8,1152,256]{2,1,0:T(8,128)(2,1)} %param.12, bf16[1,8,128,128]{2,3,1,0:T(8,128)(2,1)S(1)} %get-tuple-element.18, bf16[1,8,128,128]{2,3,1,0:T(8,128)(2,1)S(1)} %get-tuple-element.17, bf16[2,8,128,64]{2,3,1,0:T(8,128)(2,1)S(1)} %fusion.45), kind=kOutput, calls=%fused_computation.17 | convolution fusion | flops 1213497344 | bytes 6094848 | tf_op jit(solution)/shard_map/ckq,scqr->skr/dot_general | solution.py:86
  11.1 1.8 %copy.52 = bf16[2,1152,128]{2,0,1:T(2,128)(2,1)} copy(bf16[2,1152,128]{1,2,0:T(8,128)(2,1)S(1)} %fusion.16) | data formatting | bytes 1179648 | tf_op jit(solution)/shard_map/convert_element_type | solution.py:88
  12.9 6.9 %all-to-all-start = ((bf16[1,2,32,36,128]{4,1,3,0,2:T(2,128)(2,1)}), bf16[1,2,32,36,128]{4,1,3,0,2:T(2,128)(2,1)S(1)}, u32[]{:S(2)}, u32[]{:S(2)}) async-start(bf16[1,2,32,36,128]{4,1,3,0,2:T(2,128)(2,1)} %bitcast.9), calls=%async_computation | async-start | bytes 1179648 | tf_op jit(solution)/shard_map/all_to_all | solution.py:40
  19.9 0.1 copy.55
  20.0 0.1 reduce
  20.1 0.1 reshape.257
  20.3 0.1 add.172
  20.5 0.1 add.174
  20.7 0.1 add.168
  20.8 0.1 lt.103
  21.0 0.1 lt.101
  21.1 0.1 select_reduce_fusion.1
  21.2 0.1 select_reduce_fusion
  21.3 15.3 %all-to-all-done = bf16[1,2,32,36,128]{4,1,3,0,2:T(2,128)(2,1)S(1)} async-done(((bf16[1,2,32,36,128]{4,1,3,0,2:T(2,128)(2,1)}), bf16[1,2,32,36,128]{4,1,3,0,2:T(2,128)(2,1)S(1)}, u32[]{:S(2)}, u32[]{:S(2)}) %all-to-all-start) | async-done | bytes 589856 | tf_op jit(solution)/shard_map/all_to_all | solution.py:40
  36.7 0.6 copy.54
  37.3 0.4 copy.56
  37.7 0.7 gather_fusion
  38.4 0.1 copy.72
  38.5 0.3 slice_negate_fusion.1
  38.8 0.5 fusion.26
  39.3 0.4 copy.58
  39.7 0.7 gather_fusion.1
  40.4 1.3 %copy.59 = bf16[32,2,1,36,128]{4,1,3,2,0:T(2,128)(2,1)} copy(bf16[32,2,1,36,128]{4,3,1,0,2:T(8,128)(2,1)S(1)} %bitcast.112) | data formatting | bytes 1179648 | tf_op jit(solution)/shard_map/reshape | solution.py:48
  41.7 3.2 %all-to-all-start.1 = ((bf16[32,2,1,36,128]{4,1,3,2,0:T(2,128)(2,1)}), bf16[32,2,1,36,128]{4,1,3,2,0:T(2,128)(2,1)S(1)}, u32[]{:S(2)}, u32[]{:S(2)}) async-start(bf16[32,2,1,36,128]{4,1,3,2,0:T(2,128)(2,1)} %copy.59), calls=%async_computation.1 | async-start | bytes 1179648 | tf_op jit(solution)/shard_map/all_to_all | solution.py:49
  44.9 2.2 %collective-permute-start.2 = (bf16[32,128,128]{2,1,0:T(8,128)(2,1)S(1)}, bf16[32,128,128]{2,1,0:T(8,128)(2,1)S(1)}, u32[]{:S(2)}, u32[]{:S(2)}) collective-permute-start(bf16[32,128,128]{2,1,0:T(8,128)(2,1)S(1)} %copy-done.2), channel_id=1, source_target_pairs={{0,1},{1,2},{2,3},{4,5},{5,6},{6,7},{8,9},{9,10},{10,11},{12,13},{... | collective-permute-start | bytes 3145736 | tf_op jit(solution)/shard_map/ppermute | solution.py:21
  47.1 1.5 %collective-permute-start.3 = (bf16[32,128,128]{2,1,0:T(8,128)(2,1)S(1)}, bf16[32,128,128]{2,1,0:T(8,128)(2,1)}, u32[]{:S(2)}, u32[]{:S(2)}) collective-permute-start(bf16[32,128,128]{2,1,0:T(8,128)(2,1)S(1)} %copy-done.2), channel_id=1, source_target_pairs={{1,0},{2,1},{3,2},{5,4},{6,5},{7,6},{9,8},{10,9},{11,10},{13,12},{... | collective-permute-start | bytes 3145736 | tf_op jit(solution)/shard_map/ppermute | solution.py:23
  50.0 0.1 copy.63
  50.1 0.1 reshape.282
  50.2 0.6 fusion.46
  50.8 10.9 %all-to-all-done.1 = bf16[32,2,1,36,128]{4,1,3,2,0:T(2,128)(2,1)S(1)} async-done(((bf16[32,2,1,36,128]{4,1,3,2,0:T(2,128)(2,1)}), bf16[32,2,1,36,128]{4,1,3,2,0:T(2,128)(2,1)S(1)}, u32[]{:S(2)}, u32[]{:S(2)}) %all-to-all-start.1) | async-done | bytes 589856 | tf_op jit(solution)/shard_map/all_to_all | solution.py:49
  61.7 0.6 copy.62
  62.4 5.0 %fusion.57 = (bf16[2,8,128,128]{2,3,1,0:T(8,128)(2,1)}, f32[2,8,128,128]{2,3,1,0:T(8,128)}) fusion(bf16[8,128,2304]{2,1,0:T(8,128)(2,1)} %param.13, bf16[2,1152,64]{1,2,0:T(8,128)(2,1)S(1)} %get-tuple-element.14, bf16[2,1152,64]{1,2,0:T(8,128)(2,1)S(1)} %get-tuple-element.13, bf16[2,1152,128]{1,2,0:T(8,128)(2,1)S(1)} %copy.62), kind=kOutput, calls=%fused_computation.88 | convolution fusion | flops 1211760640 | bytes 7471104 | tf_op jit(solution)/shard_map/cpk,skr->scpr/dot_general | solution.py:116
  67.4 1.0 copy-done.4
  68.4 1.7 %pad_maximum_fusion = bf16[96,128,128]{2,1,0:T(8,128)(2,1)S(1)} fusion(bf16[32,128,128]{2,1,0:T(8,128)(2,1)} %collective-permute-done.3, bf16[32,128,128]{2,1,0:T(8,128)(2,1)S(1)} %copy-done.3, bf16[32,128,128]{2,1,0:T(8,128)(2,1)} %copy-done.4), kind=kLoop, calls=%fused_computation.14 | loop fusion | flops 3145728 | bytes 6291456 | tf_op jit(solution)/shard_map/concatenate | solution.py:19
  70.2 8.0 %gather_fusion.2 = bf16[192,128,128]{2,1,0:T(8,128)(2,1)} fusion(bf16[96,128,128]{2,1,0:T(8,128)(2,1)S(1)} %pad_maximum_fusion, s32[1024]{0:T(1024)S(1)} %pad_clamp_fusion), kind=kCustom, calls=%fused_computation.2 | custom fusion | bytes 12583680 | tf_op jit(solution)/shard_map/gather | solution.py:126
  78.2 8.6 %copy.64 = bf16[192,128,128]{1,2,0:T(8,128)(2,1)} copy(bf16[192,128,128]{2,1,0:T(8,128)(2,1)} %gather_fusion.2) | data formatting | bytes 12582912 | tf_op jit(solution)/shard_map/gather | solution.py:126
  86.8 6.2 %slice_negate_fusion = (bf16[32,6,128,64]{2,3,1,0:T(8,128)(2,1)}, bf16[32,6,128,64]{2,3,1,0:T(8,128)(2,1)}) fusion(bf16[32,6,128,128]{2,3,1,0:T(8,128)(2,1)} %bitcast.108), kind=kLoop, calls=%fused_computation.13 | loop fusion | flops 1572864 | bytes 12582912 | tf_op jit(solution)/shard_map/neg | solution.py:32
  93.0 1.2 %convert_element_type.34 = f32[2,8,128,128]{2,3,1,0:T(8,128)S(1)} convert(bf16[2,8,128,128]{2,3,1,0:T(8,128)(2,1)} %collective-permute-done.1) | non-fusion elementwise | flops 262144 | bytes 1572864 | tf_op jit(solution)/shard_map/convert_element_type | solution.py:117
  94.4 0.2 pad_maximum_fusion.1
  94.6 11.2 %fusion.20 = bf16[32,128,128]{1,2,0:T(8,128)(2,1)} fusion(f32[4,8,128,128]{2,3,1,0:T(8,128)S(1)} %pad_maximum_fusion.1, bf16[32,6,128,256]{3,2,1,0:T(8,128)(2,1)} %param.11, bf16[32,6,128,64]{2,3,1,0:T(8,128)(2,1)} %get-tuple-element.8, bf16[32,6,128,64]{2,3,1,0:T(8,128)(2,1)} %get-tuple-element.7, bf16[32,6,128,128]{2,3,1,0:T(8,128)(2,1)} %bitcast.109, ...), kind=kOutput, calls=%fused_computation.21 | convolution fusion | flops 1649934336 | bytes 28311584 | tf_op jit(solution)/shard_map/ienq,ieqr->inr/dot_general | solution.py:128
  105.8 2.3 %copy.65 = bf16[32,128,128]{2,1,0:T(8,128)(2,1)} copy(bf16[32,128,128]{1,2,0:T(8,128)(2,1)} %fusion.20) | data formatting | bytes 2097152 | tf_op jit(solution)/shard_map/convert_element_type | solution.py:133
  (38 shorter events, 0.7 us)
Async XLA Ops:
  0.0 38.8 %copy-start = (bf16[1,1,36,64,128]{4,3,2,1,0:T(8,128)(2,1)S(1)}, bf16[1,1,36,64,128]{4,3,2,1,0:T(8,128)(2,1)}, u32[]{:S(2)}) copy-start(bf16[1,1,36,64,128]{4,3,2,1,0:T(8,128)(2,1)} %param.14) | copy-start | bytes 1769476
  1.4 5.7 %collective-permute-start = (bf16[2,8,128,128]{2,3,1,0:T(8,128)(2,1)S(1)}, bf16[2,8,128,128]{2,3,1,0:T(8,128)(2,1)S(1)}, u32[]{:S(2)}, u32[]{:S(2)}) collective-permute-start(bf16[2,8,128,128]{2,3,1,0:T(8,128)(2,1)S(1)} %bitcast.116), channel_id=1, source_target_pairs={{0,1},{1,0},{2,3},{3,2},{4,5},{5,4},{6,7},{7,6},{8,9},{9,8},{10,11... | collective-permute-start | bytes 1572872 | tf_op jit(solution)/shard_map/ppermute | solution.py:10
  7.2 12.6 %copy-start.6 = (s32[32]{0:T(128)S(1)}, s32[32]{0:T(128)}, u32[]{:S(2)}) copy-start(s32[32]{0:T(128)} %param.9) | copy-start | bytes 388
  12.9 23.8 %all-to-all-start = ((bf16[1,2,32,36,128]{4,1,3,0,2:T(2,128)(2,1)}), bf16[1,2,32,36,128]{4,1,3,0,2:T(2,128)(2,1)S(1)}, u32[]{:S(2)}, u32[]{:S(2)}) async-start(bf16[1,2,32,36,128]{4,1,3,0,2:T(2,128)(2,1)} %bitcast.9), calls=%async_computation | async-start | bytes 1179648 | tf_op jit(solution)/shard_map/all_to_all | solution.py:40
  39.3 5.6 %copy-start.2 = (bf16[32,128,128]{2,1,0:T(8,128)(2,1)S(1)}, bf16[32,128,128]{2,1,0:T(8,128)(2,1)}, u32[]{:S(2)}) copy-start(bf16[32,128,128]{2,1,0:T(8,128)(2,1)} %param.8) | copy-start | bytes 3145732
  39.3 10.7 %copy-start.7 = (s32[32,6]{0,1:T(8,128)S(1)}, s32[32,6]{0,1:T(8,128)}, u32[]{:S(2)}) copy-start(s32[32,6]{0,1:T(8,128)} %param.10) | copy-start | bytes 2308
  41.7 20.0 %all-to-all-start.1 = ((bf16[32,2,1,36,128]{4,1,3,2,0:T(2,128)(2,1)}), bf16[32,2,1,36,128]{4,1,3,2,0:T(2,128)(2,1)S(1)}, u32[]{:S(2)}, u32[]{:S(2)}) async-start(bf16[32,2,1,36,128]{4,1,3,2,0:T(2,128)(2,1)} %copy.59), calls=%async_computation.1 | async-start | bytes 1179648 | tf_op jit(solution)/shard_map/all_to_all | solution.py:49
  44.9 22.5 %collective-permute-start.2 = (bf16[32,128,128]{2,1,0:T(8,128)(2,1)S(1)}, bf16[32,128,128]{2,1,0:T(8,128)(2,1)S(1)}, u32[]{:S(2)}, u32[]{:S(2)}) collective-permute-start(bf16[32,128,128]{2,1,0:T(8,128)(2,1)S(1)} %copy-done.2), channel_id=1, source_target_pairs={{0,1},{1,2},{2,3},{4,5},{5,6},{6,7},{8,9},{9,10},{10,11},{12,13},{... | collective-permute-start | bytes 3145736 | tf_op jit(solution)/shard_map/ppermute | solution.py:21
  47.1 21.3 %collective-permute-start.3 = (bf16[32,128,128]{2,1,0:T(8,128)(2,1)S(1)}, bf16[32,128,128]{2,1,0:T(8,128)(2,1)}, u32[]{:S(2)}, u32[]{:S(2)}) collective-permute-start(bf16[32,128,128]{2,1,0:T(8,128)(2,1)S(1)} %copy-done.2), channel_id=1, source_target_pairs={{1,0},{2,1},{3,2},{5,4},{6,5},{7,6},{9,8},{10,9},{11,10},{13,12},{... | collective-permute-start | bytes 3145736 | tf_op jit(solution)/shard_map/ppermute | solution.py:23
  62.4 6.0 %copy-start.3 = (bf16[32,128,128]{2,1,0:T(8,128)(2,1)S(1)}, bf16[32,128,128]{2,1,0:T(8,128)(2,1)}, u32[]{:S(2)}) copy-start(bf16[32,128,128]{2,1,0:T(8,128)(2,1)} %param.8) | copy-start | bytes 3145732
  67.4 25.6 %collective-permute-start.1 = (bf16[2,8,128,128]{2,3,1,0:T(8,128)(2,1)}, bf16[2,8,128,128]{2,3,1,0:T(8,128)(2,1)}, u32[]{:S(2)}, u32[]{:S(2)}) collective-permute-start(bf16[2,8,128,128]{2,3,1,0:T(8,128)(2,1)} %get-tuple-element.21), channel_id=1, source_target_pairs={{0,1},{1,0},{2,3},{3,2},{4,5},{5,4},{6,7},{7,6},{8,9},{9,8},{10,11... | collective-permute-start | bytes 1572872 | tf_op jit(solution)/shard_map/ppermute | solution.py:10
  67.4 1.0 copy-start.4
  93.0 1.4 %copy-start.5 = (f32[2,8,128,128]{2,3,1,0:T(8,128)S(1)}, f32[2,8,128,128]{2,3,1,0:T(8,128)}, u32[]{:S(2)}) copy-start(f32[2,8,128,128]{2,3,1,0:T(8,128)} %get-tuple-element.22) | copy-start | bytes 3145732
  94.6 13.4 %copy-start.1 = (bf16[1,1,36,64,128]{4,3,2,1,0:T(8,128)(2,1)S(1)}, bf16[1,1,36,64,128]{4,3,2,1,0:T(8,128)(2,1)}, u32[]{:S(2)}) copy-start(bf16[1,1,36,64,128]{4,3,2,1,0:T(8,128)(2,1)} %param.14) | copy-start | bytes 1769476
where the time goes:
time: 109 us; the launch traced here: 108 us
  local copies, waits for them, and re-layouts  32.1 us (29%)
  waiting for transfers between devices  26.2 us (24%)
  matrix products  20.6 us (19%)
  starting transfers between devices  14.4 us (13%)
  other arithmetic  10.8 us (10%)
  between operations  4.02 us (4%)
    gather x2, local copies, waits for them, and re-layouts, body(): sources = window[near_source - window_start]  16.7 us
    all_to_all x1, waiting for transfers between devices, regroup(): lax.all_to_all(shaped, ('dir', 'near'), split_axis=2, concat_axis=0, tile...  15.3 us
    dot_general x1, matrix products, body(): jnp.einsum('ienq,ieqr->inr', near_blocks, with_turned, preferred_element_...  11.2 us
    all_to_all x1, waiting for transfers between devices, collect(): lax.all_to_all(shaped, ('dir', 'near'), split_axis=0, concat_axis=2, tile...  10.9 us
    all_to_all x1, starting transfers between devices, regroup(): lax.all_to_all(shaped, ('dir', 'near'), split_axis=2, concat_axis=0, tile...  6.95 us
    neg x4, other arithmetic, turned(): -values[..., middle:]  6.54 us
    dot_general x1, matrix products, body(): jnp.einsum('cpk,skr->scpr', receive, doubled, preferred_element_type=jnp....  5.01 us
    dot_general x1, matrix products, body(): jnp.einsum('ckq,scqr->skr', aggregate, stacked, preferred_element_type=jn...  3.88 us
  transfers between devices with their start and end apart: 6, of which 2 were waited for; matrix products, arithmetic and copies ran while one was open for 33% of the time, Pallas kernels for 0%

commit v1 on v0

v1 whole, which is shorter than its diff:
```python
import functools

import jax
import jax.numpy as jnp
from jax import lax
from jax.experimental import pallas as pl
from jax.experimental.pallas import tpu as pltpu
from jax.sharding import PartitionSpec as P

MESH = pl.DeviceIdType.MESH
F32 = jnp.float32
BF16 = jnp.bfloat16


def turned(values):
    width = values.shape[-1]
    rolled = pltpu.roll(values, width // 2, values.ndim - 1)
    lane = lax.broadcasted_iota(jnp.int32, values.shape, values.ndim - 1)
    return jnp.where(lane < width // 2, -rolled, rolled)


def flipped(index, step, count):
    total = 0
    bit = 1
    while bit < count:
        total = total + bit * lax.rem(index // bit + step // bit, 2)
        bit *= 2
    return total


def kernel(
    dims,
    counts,
    near_source,
    source_blocks,
    currents,
    near_blocks,
    aggregate,
    receive,
    translations,
    out,
    own,
    borrowed,
    window,
    near_v,
    agg_v,
    rec_v,
    tra_v,
    stack,
    tile_rows,
    tile_pack,
    send1,
    recv1,
    gathered,
    incoming,
    send2,
    recv2,
    spread,
    joined,
    joined16,
    far_own,
    far_send,
    far_recv,
    near_acc,
    load_sem,
    pair_sem,
    halo_sem,
    a2a_sem,
    far_sem,
):
    dirs, nears, per, padded, slots, dirs_per_tile = dims
    devices = dirs * nears
    leaf_slots = own.shape[0]
    unknowns, channels = own.shape[1:]
    parent_slots = leaf_slots // 8
    half = parent_slots // 2
    near_per = near_v.shape[1]
    directions = agg_v.shape[1]
    dir_index = lax.axis_index("dir")
    near_index = lax.axis_index("near")
    me = dir_index * nears + near_index
    odd = lax.rem(near_index, 2)
    mate = near_index + 1 - 2 * odd
    half_leaves = half * 8

    load_own = pltpu.make_async_copy(currents, own, load_sem.at[0])
    load_agg = pltpu.make_async_copy(aggregate, agg_v, load_sem.at[1])
    load_mid = pltpu.make_async_copy(currents, window.at[pl.ds(leaf_slots, leaf_slots)], load_sem.at[2])
    load_tra = pltpu.make_async_copy(translations, tra_v, load_sem.at[3])
    load_rec = pltpu.make_async_copy(receive, rec_v, load_sem.at[4])
    load_near = pltpu.make_async_copy(near_blocks, near_v, load_sem.at[5])
    load_own.start()
    load_agg.start()

    barrier = pltpu.get_barrier_semaphore()

    def greet(step, carry):
        other = flipped(me, step, devices)
        pl.semaphore_signal(
            barrier, inc=1, device_id=(other // nears, lax.rem(other, nears)), device_id_type=MESH
        )
        return carry

    lax.fori_loop(1, devices, greet, 0)
    pl.semaphore_wait(barrier, devices - 1)

    to_mate = pltpu.make_async_remote_copy(
        src_ref=currents.at[pl.ds((1 - odd) * half_leaves, half_leaves)],
        dst_ref=borrowed,
        send_sem=pair_sem.at[0],
        recv_sem=pair_sem.at[1],
        device_id=(dir_index, mate),
        device_id_type=MESH,
    )
    to_mate.start()

    own_count = counts[me]
    mate_count = counts[dir_index * nears + mate]
    even_count = jnp.where(odd == 0, own_count, mate_count)
    load_own.wait()
    to_mate.wait_recv()
    for w in range(half):
        is_own = jnp.where(odd == 0, w < own_count, half + w >= even_count)
        own_slot = jnp.clip(jnp.where(odd == 0, w, half + w - even_count), 0, parent_slots - 1)
        mate_slot = jnp.clip(jnp.where(odd == 0, w - own_count, w), 0, half - 1)
        for c in range(8):
            mine = own[own_slot * 8 + c].astype(F32)
            theirs = borrowed[mate_slot * 8 + c].astype(F32)
            stack[pl.ds(c * unknowns, unknowns), pl.ds(w * channels, channels)] = jnp.where(
                is_own, mine, theirs
            ).astype(BF16)
    load_agg.wait()
    load_tra.start()
    load_rec.start()
    load_mid.start()
    load_near.start()

    def hop(buffer, target, other, phase):
        return pltpu.make_async_remote_copy(
            src_ref=buffer.at[other],
            dst_ref=target.at[me],
            send_sem=a2a_sem.at[phase, 0],
            recv_sem=a2a_sem.at[phase, 1],
            device_id=(other // nears, lax.rem(other, nears)),
            device_id_type=MESH,
        )

    def all_sent(buffer, phase, which):
        some = buffer.at[pl.ds(0, devices - 1)]
        pltpu.make_async_copy(some, some, a2a_sem.at[phase, which]).wait()

    message = send1.shape[1:]
    tile_devices = dirs_per_tile * nears
    tiles = devices // tile_devices
    rows = tile_devices * per
    block_rows = slots * padded

    def radiate(tile):
        start = pl.multiple_of(tile * rows, 16)
        parts = [agg_v[c, pl.ds(start, rows), :] for c in range(8)]
        real = jnp.concatenate([p[:, :unknowns] for p in parts], axis=1)
        imag = jnp.concatenate([p[:, unknowns:] for p in parts], axis=1)
        rhs = stack[...]
        real = jnp.dot(real, rhs, preferred_element_type=F32)
        imag = jnp.dot(imag, rhs, preferred_element_type=F32)
        for s in range(slots):
            lanes = slice(s * channels, (s + 1) * channels)
            tile_rows[s] = real[:, lanes] + turned(imag[:, lanes])
        for q in range(tile_devices):
            for s in range(slots):
                tile_pack[pl.ds(q * block_rows + s * padded, per), :] = tile_rows[
                    s, pl.ds(q * per, per), :
                ]
        for q in range(tile_devices):
            packed = tile_pack[pl.ds(q * block_rows, block_rows), :]
            send1[tile * tile_devices + q] = packed.reshape(message).astype(BF16)

    my_tile = me // tile_devices

    def radiate_and_send(step, carry):
        tile = flipped(my_tile, tiles - 1 - step, tiles)
        radiate(tile)
        for q in range(tile_devices):
            hop(send1, recv1, tile * tile_devices + q, 0).start()
        return carry

    lax.fori_loop(0, tiles - 1, radiate_and_send, 0)
    radiate(my_tile)
    for q in range(1, tile_devices):
        first = my_tile * tile_devices
        hop(send1, recv1, first + flipped(me - first, q, tile_devices), 0).start()
    recv1[me] = send1[me]

    def halo(side, block):
        return pltpu.make_async_remote_copy(
            src_ref=currents,
            dst_ref=window.at[pl.ds(block * leaf_slots, leaf_slots)],
            send_sem=halo_sem.at[0, block // 2],
            recv_sem=halo_sem.at[1, block // 2],
            device_id=(dir_index, near_index + side),
            device_id_type=MESH,
        )

    @pl.when(near_index < nears - 1)
    def _():
        halo(1, 0).start()

    @pl.when(near_index > 0)
    def _():
        halo(-1, 2).start()

    all_sent(recv1, 0, 1)
    load_tra.wait()
    blocks, listed, _, block_size, doubled = tra_v.shape
    block_len = block_size * padded
    for b in range(blocks):
        per_block = devices // blocks
        got = recv1[pl.ds(b * per_block, per_block)].astype(F32)
        gathered[b] = got.reshape(block_len, channels)

    def translate(k, carry):
        for b in range(blocks):
            summed = None
            for l in range(listed):
                source = 0 if blocks == 1 else source_blocks[b, l]
                rows_k = gathered[source, pl.ds(k, block_size, stride=padded), :]
                both = jnp.concatenate([rows_k, turned(rows_k)], axis=0).astype(BF16)
                part = jnp.dot(tra_v[b, l, k], both, preferred_element_type=F32)
                summed = part if summed is None else summed + part
            incoming[b, pl.ds(k, block_size, stride=padded), :] = summed
        return carry

    lax.fori_loop(0, per, translate, 0, unroll=per % 4 == 0 and per or 1)
    for b in range(blocks):
        per_block = devices // blocks
        packed = incoming[b].reshape((per_block,) + message)
        send2[pl.ds(b * per_block, per_block)] = packed.astype(BF16)

    def send_back(step, carry):
        hop(send2, recv2, flipped(me, devices - 1 - step, devices), 1).start()
        return carry

    lax.fori_loop(0, devices - 1, send_back, 0)
    recv2[me] = send2[me]

    load_mid.wait()
    load_near.wait()

    @pl.when(near_index > 0)
    def _():
        halo(1, 0).wait_recv()

    @pl.when(near_index < nears - 1)
    def _():
        halo(-1, 2).wait_recv()

    base = (me - 1) * leaf_slots

    def nearby(i, carry):
        rows_at = [near_source[i, e] - base for e in range(near_per)]
        sources = [window[jnp.clip(r, 0, 3 * leaf_slots - 1)] for r in rows_at]
        parts = [near_v[i, e] for e in range(near_per)]
        real = jnp.concatenate([p[:, :unknowns] for p in parts], axis=1)
        imag = jnp.concatenate([p[:, unknowns:] for p in parts], axis=1)
        result = jnp.dot(
            jnp.concatenate([real, imag], axis=0),
            jnp.concatenate(sources, axis=0),
            preferred_element_type=F32,
        )
        near_acc[i] = result[:unknowns] + turned(result[unknowns:])
        return carry

    lax.fori_loop(0, leaf_slots, nearby, 0)

    all_sent(recv2, 1, 1)
    load_rec.wait()
    spread[...] = recv2[...].astype(F32).reshape(spread.shape)
    for d in range(devices):
        for s in range(slots):
            joined[pl.ds(d * per, per), pl.ds(s * channels, channels)] = spread[
                pl.ds(d * block_rows + s * padded, per), :
            ]
    joined16[...] = joined[...].astype(BF16)

    def far_copy(c):
        return pltpu.make_async_remote_copy(
            src_ref=far_send.at[c],
            dst_ref=far_recv.at[c],
            send_sem=far_sem.at[0, c],
            recv_sem=far_sem.at[1, c],
            device_id=(dir_index, mate),
            device_id_type=MESH,
        )

    def absorb(c, carry):
        fields = joined16[...]
        real = jnp.dot(rec_v[c, :, pl.ds(0, directions)], fields, preferred_element_type=F32)
        imag = jnp.dot(
            rec_v[c, :, pl.ds(directions, directions)], fields, preferred_element_type=F32
        )
        for s in range(slots):
            lanes = slice(s * channels, (s + 1) * channels)
            far = real[:, lanes] + turned(imag[:, lanes])
            far_own[c, s] = far
            far_send[c, s] = far.astype(BF16)
        far_copy(c).start()
        return carry

    lax.fori_loop(0, 8, absorb, 0)

    def finish(c, carry):
        far_copy(c).wait_recv()
        for s in range(parent_slots):
            place = jnp.where(odd == 0, s, even_count + s)
            mine_at = place - half * odd
            mine = (mine_at >= 0) & (mine_at < half)
            own_at = jnp.clip(mine_at, 0, half - 1)
            mate_at = jnp.clip(place - half * (1 - odd), 0, half - 1)
            theirs = far_recv[c, 0]
            for w in range(1, half):
                theirs = jnp.where(mate_at == w, far_recv[c, w], theirs)
            far = jnp.where(mine, far_own[c, own_at], theirs.astype(F32))
            total = far + near_acc[s * 8 + c]
            out[s * 8 + c] = jnp.where(s < own_count, total, 0.0).astype(BF16)
        return carry

    lax.fori_loop(0, 8, finish, 0)

    to_mate.wait_send()
    all_sent(send1, 0, 0)
    all_sent(send2, 1, 0)
    for c in range(8):
        far_copy(c).wait_send()

    @pl.when(near_index < nears - 1)
    def _():
        halo(1, 0).wait_send()

    @pl.when(near_index > 0)
    def _():
        halo(-1, 2).wait_send()


def body(
    currents, counts, near_source, near_blocks, aggregate, receive, translations, source_blocks
):
    dirs, nears = lax.axis_size("dir"), lax.axis_size("near")
    devices = dirs * nears
    leaf_slots, unknowns, channels = currents.shape
    parent_slots = leaf_slots // 8
    slots = parent_slots // 2
    blocks, listed, per, block_size, doubled = translations.shape
    directions = aggregate.shape[1]
    padded = -(-per * slots // 8) * 8 // slots
    dirs_per_tile = 1
    while dirs_per_tile * nears * per % 16:
        dirs_per_tile *= 2
    rows = dirs_per_tile * nears * per
    message = (slots * padded // 8, 8, channels)
    exchange = pltpu.VMEM((devices,) + message, BF16)
    any_spec = pl.BlockSpec(memory_space=pl.ANY)
    smem_spec = pl.BlockSpec(memory_space=pltpu.SMEM)
    return pl.pallas_call(
        functools.partial(kernel, (dirs, nears, per, padded, slots, dirs_per_tile)),
        out_shape=jax.ShapeDtypeStruct(currents.shape, BF16),
        in_specs=[smem_spec] * 3 + [any_spec] * 5,
        out_specs=pl.BlockSpec(memory_space=pltpu.VMEM),
        scratch_shapes=[
            pltpu.VMEM(currents.shape, BF16),
            pltpu.VMEM((slots * 8, unknowns, channels), BF16),
            pltpu.VMEM((3 * leaf_slots, unknowns, channels), BF16),
            pltpu.VMEM(near_blocks.shape, BF16),
            pltpu.VMEM(aggregate.shape, BF16),
            pltpu.VMEM(receive.shape, BF16),
            pltpu.VMEM(translations.shape, BF16),
            pltpu.VMEM((8 * unknowns, slots * channels), BF16),
            pltpu.VMEM((slots, rows, channels), F32),
            pltpu.VMEM((dirs_per_tile * nears * slots * padded, channels), F32),
            exchange,
            exchange,
            pltpu.VMEM((blocks, block_size * padded, channels), F32),
            pltpu.VMEM((blocks, block_size * padded, channels), F32),
            exchange,
            exchange,
            pltpu.VMEM((devices * slots * padded, channels), F32),
            pltpu.VMEM((directions, slots * channels), F32),
            pltpu.VMEM((directions, slots * channels), BF16),
            pltpu.VMEM((8, slots, unknowns, channels), F32),
            pltpu.VMEM((8, slots, unknowns, channels), BF16),
            pltpu.VMEM((8, slots, unknowns, channels), BF16),
            pltpu.VMEM((leaf_slots, unknowns, channels), F32),
            pltpu.SemaphoreType.DMA((6,)),
            pltpu.SemaphoreType.DMA((2,)),
            pltpu.SemaphoreType.DMA((2, 2)),
            pltpu.SemaphoreType.DMA((2, 2)),
            pltpu.SemaphoreType.DMA((2, 8)),
        ],
        compiler_params=pltpu.CompilerParams(
            collective_id=0, has_side_effects=True, vmem_limit_bytes=60 * 2**20
        ),
    )(
        counts,
        near_source,
        source_blocks,
        currents,
        near_blocks,
        aggregate,
        receive,
        translations,
    )


def solution(mesh):
    return jax.shard_map(
        body,
        mesh=mesh,
        in_specs=(
            P(("dir", "near"), None, None),
            P(),
            P(("dir", "near"), None),
            P(("dir", "near"), None, None, None),
            P(),
            P(),
            P(None, None, ("dir", "near"), None, None),
            P(),
        ),
        out_specs=P(("dir", "near"), None, None),
        check_vma=False,
    )
```

time: 109 us -> 58.4 us (0.54)
  Pallas kernels: 0 us -> 53.1 us
  local copies, waits for them, and re-layouts: 32.1 us -> 3.68 us
  waiting for transfers between devices: 26.2 us -> 0 us
  matrix products: 20.6 us -> 0 us
  starting transfers between devices: 14.4 us -> 0 us
  other arithmetic: 10.8 us -> 0 us
  between operations: 4.02 us -> 0.66 us
    pallas_call x0 -> x1, Pallas kernels: none -> 53.1 us  [body(): pl.pallas_call(functools.partial(kernel, (dirs, nears, per, padded, slots...]
    all_to_all x2 -> x0, waiting for transfers between devices: 26.2 us -> none  [the longest x1 15.3 us: regroup(): lax.all_to_all(shaped, ('dir', 'near'), split_axis=2, concat_axis=0, tile...]
    dot_general x4 -> x0, matrix products: 20.6 us -> none  [the longest x1 11.2 us: body(): jnp.einsum('ienq,ieqr->inr', near_blocks, with_turned, preferred_element_...]
    gather x5 -> x0, local copies, waits for them, and re-layouts: 18.2 us -> none  [the longest x2 16.7 us: body(): sources = window[near_source - window_start]]
    all_to_all x2 -> x0, starting transfers between devices: 10.1 us -> none  [the longest x1 6.95 us: regroup(): lax.all_to_all(shaped, ('dir', 'near'), split_axis=2, concat_axis=0, tile...]
    neg x4 -> x0, other arithmetic: 6.54 us -> none  [turned(): -values[..., middle:]]
    ppermute x4 -> x0, starting transfers between devices: 4.25 us -> none  [the longest x1 2.22 us: padded(): lax.ppermute(tail, axis, [(i, (i + 1) % count) for i in range(ends)])]
    convert_element_type x2 -> x0, local copies, waits for them, and re-layouts: 4.02 us -> none  [the longest x1 2.26 us: body(): return jnp.where(is_live[:, None, None], summed, 0.0).astype(jnp.bfloat16)]
  transfers between devices with their start and end apart: 6 -> 0, of which waited for: 2 -> 0; matrix products, arithmetic and copies ran while one was open for 33% -> 0% of each run, Pallas kernels for 0% -> 0%
where the time goes in v1:
time: 58.4 us; the launch traced here: 57.4 us
  Pallas kernels  53.1 us (91%)
  local copies, waits for them, and re-layouts  3.68 us (6%)
  between operations  0.66 us (1%)
    pallas_call x1, Pallas kernels, body(): pl.pallas_call(functools.partial(kernel, (dirs, nears, per, padded, slots...  53.1 us
    unnamed x2, local copies, waits for them, and re-layouts  3.68 us

profile of v1, /device:TPU:0, one launch (start us, length us, event | category | flops | bytes accessed | tf_op | source)
XLA Modules:
  0.0 57.4 jit_solution(9620994859659896126)
XLA Ops:
  0.7 1.4 %copy.9.near_source = s32[32,6]{1,0:T(8,128)} copy(s32[32,6]{0,1:T(8,128)} %param.10) | data formatting | bytes 1536 | tf_op args[2]
  2.0 53.1 %shard_map.82 = bf16[32,128,128]{2,1,0:T(8,128)(2,1)} custom-call(s32[32]{0:T(128)} %counts.1, s32[32,6]{1,0:T(8,128)} %copy.9.near_source, s32[1,1]{1,0:T(1,128)S(6)} %copy.11.source_blocks, bf16[32,128,128]{2,1,0:T(8,128)(2,1)} %currents.1, bf16[32,6,128,256]{3,2,1,0:T(8,128)(2,1)} %near_blocks.1, bf16[8,1152,256]{2,1,0:T(8,128)(2,1)} %aggregate.1, ...), custom_call_target="tpu_custom_call" | custom-call | tf_op jit(solution)/shard_map/pallas_call | solution.py:363
  55.1 2.3 %copy.12 = bf16[32,128,128]{2,1,0:T(8,128)(2,1)} copy(bf16[32,128,128]{2,1,0:T(8,128)(2,1)} %shard_map.82) | data formatting | bytes 2097152

commit v2 on v1

--- a/solution.py
+++ b/solution.py
@@ -89,8 +89,19 @@
     load_tra = pltpu.make_async_copy(translations, tra_v, load_sem.at[3])
     load_rec = pltpu.make_async_copy(receive, rec_v, load_sem.at[4])
     load_near = pltpu.make_async_copy(near_blocks, near_v, load_sem.at[5])
+
+    def start_pieces(source, target, sem, pieces):
+        size = target.shape[0] // pieces
+        for piece in range(pieces):
+            cut = pl.ds(piece * size, size)
+            pltpu.make_async_copy(source.at[cut], target.at[cut], sem).start()
+
     load_own.start()
-    load_agg.start()
+    start_pieces(aggregate, agg_v, load_sem.at[1], 8)
+    load_tra.start()
+    load_mid.start()
+    start_pieces(near_blocks, near_v, load_sem.at[5], 8)
+    start_pieces(receive, rec_v, load_sem.at[4], 8)
 
     barrier = pltpu.get_barrier_semaphore()
 
@@ -113,6 +124,24 @@
         device_id_type=MESH,
     )
     to_mate.start()
+
+    def halo(side, block):
+        return pltpu.make_async_remote_copy(
+            src_ref=currents,
+            dst_ref=window.at[pl.ds(block * leaf_slots, leaf_slots)],
+            send_sem=halo_sem.at[0, block // 2],
+            recv_sem=halo_sem.at[1, block // 2],
+            device_id=(dir_index, near_index + side),
+            device_id_type=MESH,
+        )
+
+    @pl.when(near_index < nears - 1)
+    def _():
+        halo(1, 0).start()
+
+    @pl.when(near_index > 0)
+    def _():
+        halo(-1, 2).start()
 
     own_count = counts[me]
     mate_count = counts[dir_index * nears + mate]
@@ -130,10 +159,6 @@
                 is_own, mine, theirs
             ).astype(BF16)
     load_agg.wait()
-    load_tra.start()
-    load_rec.start()
-    load_mid.start()
-    load_near.start()
 
     def hop(buffer, target, other, phase):
         return pltpu.make_async_remote_copy(
@@ -191,24 +216,6 @@
         hop(send1, recv1, first + flipped(me - first, q, tile_devices), 0).start()
     recv1[me] = send1[me]
 
-    def halo(side, block):
-        return pltpu.make_async_remote_copy(
-            src_ref=currents,
-            dst_ref=window.at[pl.ds(block * leaf_slots, leaf_slots)],
-            send_sem=halo_sem.at[0, block // 2],
-            recv_sem=halo_sem.at[1, block // 2],
-            device_id=(dir_index, near_index + side),
-            device_id_type=MESH,
-        )
-
-    @pl.when(near_index < nears - 1)
-    def _():
-        halo(1, 0).start()
-
-    @pl.when(near_index > 0)
-    def _():
-        halo(-1, 2).start()
-
     all_sent(recv1, 0, 1)
     load_tra.wait()
     blocks, listed, _, block_size, doubled = tra_v.shape
@@ -257,7 +264,7 @@
     base = (me - 1) * leaf_slots
 
     def nearby(i, carry):
-        rows_at = [near_source[i, e] - base for e in range(near_per)]
+        rows_at = [near_source[e, i] - base for e in range(near_per)]
         sources = [window[jnp.clip(r, 0, 3 * leaf_slots - 1)] for r in rows_at]
         parts = [near_v[i, e] for e in range(near_per)]
         real = jnp.concatenate([p[:, :unknowns] for p in parts], axis=1)
@@ -400,7 +407,7 @@
         ),
     )(
         counts,
-        near_source,
+        near_source.T,
         source_blocks,
         currents,
         near_blocks,

time: 58.4 us -> 51.7 us (0.89); the launches traced: 57.4 us -> 51.5 us
  Pallas kernels: 53.1 us -> 48.6 us
  local copies, waits for them, and re-layouts: 3.68 us -> 2.31 us
    pallas_call x1, Pallas kernels: 53.1 us -> 48.6 us  [body(): pl.pallas_call(functools.partial(kernel, (dirs, nears, per, padded, slots...]
    unnamed x2 -> x1, local copies, waits for them, and re-layouts: 3.68 us -> 2.31 us
where the time goes in v2:
time: 51.7 us; the launch traced here: 51.5 us
  Pallas kernels  48.6 us (94%)
  local copies, waits for them, and re-layouts  2.31 us (4%)
  between operations  0.66 us (1%)
    pallas_call x1, Pallas kernels, body(): pl.pallas_call(functools.partial(kernel, (dirs, nears, per, padded, slots...  48.6 us
    unnamed x1, local copies, waits for them, and re-layouts  2.31 us

profile of v2, /device:TPU:0, one launch (start us, length us, event | category | flops | bytes accessed | tf_op | source)
XLA Modules:
  0.0 51.5 jit_solution(4857864098287643674)
XLA Ops:
  0.7 48.6 %shard_map.82 = bf16[32,128,128]{2,1,0:T(8,128)(2,1)} custom-call(s32[32]{0:T(128)} %counts.1, s32[6,32]{1,0:T(8,128)} %bitcast.1, s32[1,1]{1,0:T(1,128)S(6)} %copy.10.source_blocks, bf16[32,128,128]{2,1,0:T(8,128)(2,1)} %currents.1, bf16[32,6,128,256]{3,2,1,0:T(8,128)(2,1)} %near_blocks.1, bf16[8,1152,256]{2,1,0:T(8,128)(2,1)} %aggregate.1, ...), custom_call_target="tpu_custom_call" | custom-call | tf_op jit(solution)/shard_map/pallas_call | solution.py:370
  49.2 2.3 %copy.11 = bf16[32,128,128]{2,1,0:T(8,128)(2,1)} copy(bf16[32,128,128]{2,1,0:T(8,128)(2,1)} %shard_map.82) | data formatting | bytes 2097152

commit v3 on v2

--- a/solution.py
+++ b/solution.py
@@ -106,13 +106,13 @@
     barrier = pltpu.get_barrier_semaphore()
 
     def greet(step, carry):
-        other = flipped(me, step, devices)
+        other = flipped(me, devices - step, devices)
         pl.semaphore_signal(
             barrier, inc=1, device_id=(other // nears, lax.rem(other, nears)), device_id_type=MESH
         )
         return carry
 
-    lax.fori_loop(1, devices, greet, 0)
+    lax.fori_loop(1, devices, greet, 0, unroll=True)
     pl.semaphore_wait(barrier, devices - 1)
 
     to_mate = pltpu.make_async_remote_copy(
@@ -247,7 +247,7 @@
         hop(send2, recv2, flipped(me, devices - 1 - step, devices), 1).start()
         return carry
 
-    lax.fori_loop(0, devices - 1, send_back, 0)
+    lax.fori_loop(0, devices - 1, send_back, 0, unroll=True)
     recv2[me] = send2[me]
 
     load_mid.wait()

time: 51.7 us -> 51.4 us (level)
  no operation moved by 1% of the time
where the time goes in v3:
time: 51.4 us; the launch traced here: 51.2 us
  Pallas kernels  48.2 us (94%)
  local copies, waits for them, and re-layouts  2.31 us (4%)
  between operations  0.66 us (1%)
    pallas_call x1, Pallas kernels, body(): pl.pallas_call(functools.partial(kernel, (dirs, nears, per, padded, slots...  48.2 us
    unnamed x1, local copies, waits for them, and re-layouts  2.31 us

profile of v3, /device:TPU:0, one launch (start us, length us, event | category | flops | bytes accessed | tf_op | source)
XLA Modules:
  0.0 51.2 jit_solution(12416340747502080272)
XLA Ops:
  0.7 48.2 %shard_map.82 = bf16[32,128,128]{2,1,0:T(8,128)(2,1)} custom-call(s32[32]{0:T(128)} %counts.1, s32[6,32]{1,0:T(8,128)} %bitcast.1, s32[1,1]{1,0:T(1,128)S(6)} %copy.10.source_blocks, bf16[32,128,128]{2,1,0:T(8,128)(2,1)} %currents.1, bf16[32,6,128,256]{3,2,1,0:T(8,128)(2,1)} %near_blocks.1, bf16[8,1152,256]{2,1,0:T(8,128)(2,1)} %aggregate.1, ...), custom_call_target="tpu_custom_call" | custom-call | tf_op jit(solution)/shard_map/pallas_call | solution.py:370
  48.9 2.3 %copy.11 = bf16[32,128,128]{2,1,0:T(8,128)(2,1)} copy(bf16[32,128,128]{2,1,0:T(8,128)(2,1)} %shard_map.82) | data formatting | bytes 2097152
